TPU v7x, 512 devices: a whole 4x4x16 slice. The times are simulated.
512 devices in a mesh: dp: 32 (over x, y, z_hi), seq: 16 (over z_lo, core).
Axes of the slice: x: 4, y: 4, z: 16 (z_hi: 2, z_lo: 8; z = z_hi * 8 + z_lo), core: 2. Of those that a mesh axis runs over, the one named last changes fastest.
Arguments:
- tokens: bfloat16 [32, 2048, 2048], P('dp', 'seq'), may hold values from -60 to 60
- master: float32 [2048, 3072], P('dp', 'seq'), may hold values from -0.21875 to 0.21875
- moment_one: float32 [2048, 3072], P('dp', 'seq'), may hold values from -0.06 to 0.06
- moment_two: float32 [2048, 3072], P('dp', 'seq'), may hold values from 1e-05 to 0.0001
- gradient: float32 [2048, 3072], P('dp', 'seq'), may hold values from -0.6 to 0.6
Outputs:
- context: bfloat16 [32, 2048, 2048], P('dp', 'seq')
- new_master: float32 [2048, 3072], P('dp', 'seq')
All inputs are finite; a program needn't handle non-finite values.
Results may differ from a plain program's by a relative error of at most 0.013.
The roundings to bfloat16 on the way count: a program that leaves them out, or rounds other values in their place, can miss the bound.
Values may be sent and summed in bfloat16 or wider, within the bound.
A program may use at most 64 MiB of HBM per device.

v0:
```python
import math

import jax
import jax.numpy as jnp
from jax import lax
from jax.sharding import PartitionSpec as P

HEADS = 16
KV_HEADS = 4
HEAD_DIM = 128


beta_one = 0.9
beta_two = 0.999
learn_rate = 0.005
decay_rate = 0.1
adam_eps = 1e-08
rope_theta = 500000.0
correct_one = 1.0 - math.exp(1000.0 * math.log(beta_one))
correct_two = 1.0 - math.exp(1000.0 * math.log(beta_two))


def adam_step(master, moment_one, moment_two, gradient):
    first = beta_one * moment_one + (1.0 - beta_one) * gradient
    second = beta_two * moment_two + (1.0 - beta_two) * gradient * gradient
    update = first / correct_one / (jnp.sqrt(second / correct_two) + adam_eps)
    return master - learn_rate * (update + decay_rate * master)


def rotate_pairs(heads_in, positions):
    half_width = heads_in.shape[-1] // 2
    frequency = rope_theta ** (
        -(jnp.arange(half_width).astype(jnp.float32) * 2.0) / heads_in.shape[-1]
    )
    angles = positions[:, None] * frequency[None, :]
    cosine = jnp.cos(angles)[:, None, :]
    sine = jnp.sin(angles)[:, None, :]
    lower_half = heads_in[..., :half_width]
    upper_half = heads_in[..., half_width:]
    return jnp.concatenate(
        [lower_half * cosine - upper_half * sine, upper_half * cosine + lower_half * sine], axis=-1
    )


def split_heads(projected, positions):
    row_count = projected.shape[0]
    query_width = HEADS * HEAD_DIM
    key_width = KV_HEADS * HEAD_DIM
    queries = projected[:, :query_width].reshape(row_count, HEADS, HEAD_DIM)
    key_heads = projected[:, query_width : query_width + key_width].reshape(
        row_count, KV_HEADS, HEAD_DIM
    )
    value_heads = projected[:, query_width + key_width :].reshape(row_count, KV_HEADS, HEAD_DIM)
    queries = rotate_pairs(queries, positions).astype(jnp.bfloat16)
    key_heads = rotate_pairs(key_heads, positions).astype(jnp.bfloat16)
    return (queries, key_heads, value_heads.astype(jnp.bfloat16))


def attend(queries, key_rows, value_rows):
    length = queries.shape[0]
    block_rows = 512
    score_scale = 1.0 / math.sqrt(queries.shape[-1])
    outputs = []
    for block_start in range(0, length, block_rows):
        key_end = block_start + block_rows
        scores = (
            jnp.einsum(
                "qhd,khd->hqk",
                queries[block_start:key_end],
                key_rows[:key_end],
                preferred_element_type=jnp.float32,
            )
            * score_scale
        )
        allowed = (block_start + jnp.arange(block_rows))[:, None] >= jnp.arange(key_end)[None, :]
        scores = jnp.where(allowed[None], scores, -jnp.inf)
        row_top = jnp.max(scores, axis=-1, keepdims=True)
        exponent = jnp.exp(scores - row_top)
        probabilities = (exponent / jnp.sum(exponent, axis=-1, keepdims=True)).astype(jnp.bfloat16)
        block_out = jnp.einsum(
            "hqk,khd->qhd", probabilities, value_rows[:key_end], preferred_element_type=jnp.float32
        )
        outputs.append(block_out.astype(jnp.bfloat16))
    return jnp.concatenate(outputs, axis=0)


def shards(tokens, master, moment_one, moment_two, gradient):
    new_master = adam_step(master, moment_one, moment_two, gradient)
    weights_bf = new_master.astype(jnp.bfloat16)
    inputs = tokens[0]
    rows_here = inputs.shape[0]
    columns = lax.all_gather(weights_bf, "seq", axis=1, tiled=True)
    full_weights = lax.all_gather(columns, "dp", axis=0, tiled=True)
    projected = jnp.dot(inputs, full_weights, preferred_element_type=jnp.float32)
    seq_index = lax.axis_index("seq")
    positions = (seq_index * rows_here + jnp.arange(rows_here)).astype(jnp.float32)
    queries, key_heads, value_heads = split_heads(projected, positions)
    group_size = HEADS // KV_HEADS
    key_wide = jnp.repeat(key_heads, group_size, axis=1)
    value_wide = jnp.repeat(value_heads, group_size, axis=1)
    queries_all, keys_all, values_all = (
        lax.all_to_all(queries, "seq", split_axis=1, concat_axis=0, tiled=True),
        lax.all_to_all(key_wide, "seq", split_axis=1, concat_axis=0, tiled=True),
        lax.all_to_all(value_wide, "seq", split_axis=1, concat_axis=0, tiled=True),
    )
    context = attend(queries_all, keys_all, values_all)
    returned = lax.all_to_all(context, "seq", split_axis=0, concat_axis=1, tiled=True)
    return (returned.reshape(1, rows_here, HEADS * HEAD_DIM), new_master)


def solution(mesh):
    placed = (P("dp", "seq", None), P("dp", "seq"), P("dp", "seq"), P("dp", "seq"), P("dp", "seq"))
    return jax.shard_map(
        shards,
        mesh=mesh,
        in_specs=placed,
        out_specs=(P("dp", "seq", None), P("dp", "seq")),
        check_vma=False,
    )
```

profile of v0, /device:TPU:1, one launch (start us, length us, event | category | flops | bytes accessed | tf_op | source)
XLA Modules:
  0.0 543.9 jit_solution(13772782266259674989)
XLA Ops:
  7.2 1.7 convert_bitcast_fusion
  8.9 39.9 %all-gather = bf16[16,192,64]{1,2,0:T(8,128)(2,1)S(1)} all-gather(bf16[1,192,64]{1,2,0:T(8,128)(2,1)S(1)} %get-tuple-element.6), channel_id=1, replica_groups=mesh['dp'=32,'seq'=16] {'seq'}, dimensions={0}, use_global_device_ids=true | all-gather | bytes 417792 | tf_op jit(solution)/shard_map/all_gather | solution.py:92
  48.8 0.3 copy.45
  49.1 1.3 reshape.254
  50.5 0.2 multiply_cosine_fusion
  50.7 309.3 %all-gather.3.cloned.1.call-done = bf16[2048,3072]{1,0:T(8,128)(2,1)} async-done(((bf16[64,3072]{1,0:T(8,128)(2,1)}), bf16[2048,3072]{1,0:T(8,128)(2,1)}) %all-gather.3.cloned.1.call-update) | async-done | bytes 12582928 | tf_op jit(solution)/shard_map/all_gather | solution.py:93
  360.0 6.5 %convolution_bitcast_fusion = f32[128,3072]{0,1:T(8,128)S(1)} fusion(bf16[2048,3072]{1,0:T(8,128)(2,1)} %all-gather.3.cloned.1.call-done, bf16[1,128,2048]{2,1,0:T(8,128)(2,1)S(1)} %copy-done), kind=kOutput, calls=%fused_computation.4 | convolution fusion | flops 1610612736 | bytes 14680064 | tf_op jit(solution)/shard_map/dot_general | solution.py:94
  366.6 0.1 copy.51
  366.7 0.9 broadcast_in_dim.18
  367.6 29.8 %all-to-all-start.2 = ((bf16[128,16,128]{2,0,1:T(8,128)(2,1)}), bf16[128,16,128]{2,0,1:T(8,128)(2,1)S(1)}, u32[]{:S(2)}, u32[]{:S(2)}) async-start(bf16[128,16,128]{2,0,1:T(8,128)(2,1)} %bitcast.15), calls=%async_computation.2 | async-start | bytes 1048576 | tf_op jit(solution)/shard_map/all_to_all | solution.py:103
  397.5 0.1 copy.46
  397.6 26.1 %all-to-all-done.2 = bf16[128,16,128]{2,0,1:T(8,128)(2,1)S(1)} async-done(((bf16[128,16,128]{2,0,1:T(8,128)(2,1)}), bf16[128,16,128]{2,0,1:T(8,128)(2,1)S(1)}, u32[]{:S(2)}, u32[]{:S(2)}) %all-to-all-start.2) | async-done | bytes 524320 | tf_op jit(solution)/shard_map/all_to_all | solution.py:103
  423.7 0.9 broadcast_in_dim.17
  424.6 7.1 %all-to-all-start = ((bf16[128,16,128]{2,0,1:T(8,128)(2,1)}), bf16[128,16,128]{2,0,1:T(8,128)(2,1)}, u32[]{:S(2)}, u32[]{:S(2)}) async-start(bf16[128,16,128]{2,0,1:T(8,128)(2,1)} %bitcast.6), calls=%async_computation | async-start | bytes 1048576 | tf_op jit(solution)/shard_map/all_to_all | solution.py:104
  431.6 0.1 copy.48
  431.7 0.1 copy.50
  431.8 0.1 slice.81
  431.9 0.9 fusion.21
  432.8 0.3 copy.56
  433.1 1.4 copy.57
  434.5 0.3 subtract_convert_fusion
  434.8 1.1 pad_maximum_fusion
  435.9 22.0 %all-to-all-done = bf16[128,16,128]{2,0,1:T(8,128)(2,1)} async-done(((bf16[128,16,128]{2,0,1:T(8,128)(2,1)}), bf16[128,16,128]{2,0,1:T(8,128)(2,1)}, u32[]{:S(2)}, u32[]{:S(2)}) %all-to-all-start) | async-done | bytes 524320 | tf_op jit(solution)/shard_map/all_to_all | solution.py:104
  458.0 7.1 %all-to-all-start.1 = ((bf16[128,16,128]{2,0,1:T(8,128)(2,1)}), bf16[128,16,128]{2,0,1:T(8,128)(2,1)S(1)}, u32[]{:S(2)}, u32[]{:S(2)}) async-start(bf16[128,16,128]{2,0,1:T(8,128)(2,1)} %pad_maximum_fusion), calls=%async_computation.1 | async-start | bytes 1048576 | tf_op jit(solution)/shard_map/all_to_all | solution.py:102
  465.1 0.9 slice.80
  466.0 1.0 slice.89
  467.0 1.0 slice.92
  468.0 23.2 %all-to-all-done.1 = bf16[128,16,128]{2,0,1:T(8,128)(2,1)S(1)} async-done(((bf16[128,16,128]{2,0,1:T(8,128)(2,1)}), bf16[128,16,128]{2,0,1:T(8,128)(2,1)S(1)}, u32[]{:S(2)}, u32[]{:S(2)}) %all-to-all-start.1) | async-done | bytes 524320 | tf_op jit(solution)/shard_map/all_to_all | solution.py:102
  491.3 0.3 fusion.26
  491.6 0.2 fusion.13
  491.8 0.3 fusion.9
  492.2 0.6 fusion.25
  492.7 0.5 fusion.4
  493.2 0.7 fusion.11
  493.9 0.8 fusion.24
  494.7 0.6 fusion.2
  495.3 0.9 fusion.12
  496.2 1.0 fusion.23
  497.2 0.7 fusion
  497.9 2.2 fusion.10
  500.1 0.5 broadcast.113
  500.6 1.0 reduce.16
  501.6 0.3 copy.58
  501.9 0.1 reshape.255
  502.0 33.1 %all_to_all.60 = bf16[16,2,8192]{2,1,0:T(2,128)(2,1)S(1)} all-to-all(bf16[16,2,8192]{2,1,0:T(2,128)(2,1)S(1)} %reshape.255), channel_id=1, replica_groups=mesh['dp'=32,'seq'=16] {'seq'}, dimensions={0} | all-to-all | bytes 1048576 | tf_op jit(solution)/shard_map/all_to_all | solution.py:107
  535.1 0.5 reshape.256
  535.7 0.3 copy.53
  536.0 1.0 copy.54
  (19 shorter events, 0.4 us)
Async XLA Ops:
  7.2 352.8 %copy-start = (bf16[1,128,2048]{2,1,0:T(8,128)(2,1)S(1)}, bf16[1,128,2048]{2,1,0:T(8,128)(2,1)}, u32[]{:S(2)}) copy-start(bf16[1,128,2048]{2,1,0:T(8,128)(2,1)} %param.5) | copy-start | bytes 1572868
  7.2 352.8 %all-gather.3.cloned.1.call-start = ((), (), s32[]{:S(2)}) async-start(), calls=%async_computation.4 | async-start | bytes 12976128 | tf_op jit(solution)/shard_map/all_gather | solution.py:93
  367.6 56.1 %all-to-all-start.2 = ((bf16[128,16,128]{2,0,1:T(8,128)(2,1)}), bf16[128,16,128]{2,0,1:T(8,128)(2,1)S(1)}, u32[]{:S(2)}, u32[]{:S(2)}) async-start(bf16[128,16,128]{2,0,1:T(8,128)(2,1)} %bitcast.15), calls=%async_computation.2 | async-start | bytes 1048576 | tf_op jit(solution)/shard_map/all_to_all | solution.py:103
  424.6 33.4 %all-to-all-start = ((bf16[128,16,128]{2,0,1:T(8,128)(2,1)}), bf16[128,16,128]{2,0,1:T(8,128)(2,1)}, u32[]{:S(2)}, u32[]{:S(2)}) async-start(bf16[128,16,128]{2,0,1:T(8,128)(2,1)} %bitcast.6), calls=%async_computation | async-start | bytes 1048576 | tf_op jit(solution)/shard_map/all_to_all | solution.py:104
  458.0 33.3 %all-to-all-start.1 = ((bf16[128,16,128]{2,0,1:T(8,128)(2,1)}), bf16[128,16,128]{2,0,1:T(8,128)(2,1)S(1)}, u32[]{:S(2)}, u32[]{:S(2)}) async-start(bf16[128,16,128]{2,0,1:T(8,128)(2,1)} %pad_maximum_fusion), calls=%async_computation.1 | async-start | bytes 1048576 | tf_op jit(solution)/shard_map/all_to_all | solution.py:102
Sparse Core Ops, SparseCore 0:
  50.6 309.3 all-gather.2
where the time goes:
time: 545 us; the launch traced here: 544 us
  waiting for transfers between devices  381 us (70%)
  blocking collectives  73 us (13%)
  starting transfers between devices  44 us (8%)
  between operations  14.3 us (3%)
  matrix products  13.2 us (2%)
  local copies, waits for them, and re-layouts  12.3 us (2%)
  other arithmetic  6.39 us (1%)
    all_gather x1, waiting for transfers between devices, shards(): full_weights = lax.all_gather(columns, 'dp', axis=0, tiled=True)  309 us
    all_gather x1, blocking collectives, shards(): columns = lax.all_gather(weights_bf, 'seq', axis=1, tiled=True)  39.9 us
    all_to_all x1, blocking collectives, shards(): lax.all_to_all(context, 'seq', split_axis=0, concat_axis=1, tiled=True)  33.1 us
    all_to_all x1, starting transfers between devices, shards(): lax.all_to_all(key_wide, 'seq', split_axis=1, concat_axis=0, tiled=True)  29.8 us
    all_to_all x1, waiting for transfers between devices, shards(): lax.all_to_all(key_wide, 'seq', split_axis=1, concat_axis=0, tiled=True)  26.1 us
    all_to_all x1, waiting for transfers between devices, shards(): lax.all_to_all(queries, 'seq', split_axis=1, concat_axis=0, tiled=True)  23.2 us
    all_to_all x1, waiting for transfers between devices, shards(): lax.all_to_all(value_wide, 'seq', split_axis=1, concat_axis=0, tiled=True)  22 us
  transfers between devices with their start and end apart: 4, of which 4 were waited for; matrix products, arithmetic and copies ran while one was open for 1% of the time, Pallas kernels for 0%

commit v1 on v0

v1 whole, which is shorter than its diff:
```python
import functools
import math

import jax
import jax.numpy as jnp
from jax import lax
from jax.experimental import pallas as pl
from jax.experimental.pallas import tpu as pltpu
from jax.sharding import PartitionSpec as P

HEADS = 16
KV_HEADS = 4
HEAD_DIM = 128
SIDE = 4
LINE = 8
RING = 16
MESH = pl.DeviceIdType.MESH

beta_one = 0.9
beta_two = 0.999
learn_rate = 0.005
decay_rate = 0.1
adam_eps = 1e-08
rope_theta = 500000.0
correct_one = 1.0 - math.exp(1000.0 * math.log(beta_one))
correct_two = 1.0 - math.exp(1000.0 * math.log(beta_two))

SCALE = 1.0 / math.sqrt(HEAD_DIM)
BLK = 128
SUB = 64
ROWS = 128
GROUPS = ((1024, 256, True), (1280, 256, False), (0, 512, True), (512, 512, False))


def adam_step(master, moment_one, moment_two, gradient):
    first = beta_one * moment_one + (1.0 - beta_one) * gradient
    second = beta_two * moment_two + (1.0 - beta_two) * gradient * gradient
    update = first / correct_one / (jnp.sqrt(second / correct_two) + adam_eps)
    return master - learn_rate * (update + decay_rate * master)


def kernel(
    tokens, shard, cos, sin, out,
    other, blk, W, tok, kv, q, acc, top, total, ctx,
    misc, zsend, zrecv, s1send, s1recv, s2send, s2recv, kvsend, kvrecv,
):
    dp, seq = lax.axis_index("dp"), lax.axis_index("seq")
    zh = lax.rem(dp, 2)
    xy = lax.div(dp, 2)
    x, y = lax.div(xy, SIDE), lax.rem(xy, SIDE)
    c = lax.rem(seq, 2)
    zl = lax.div(seq, 2)
    z = zh * LINE + zl

    def at(xx, yy, zz, cc):
        return {
            "dp": (xx * SIDE + yy) * 2 + lax.div(zz, LINE),
            "seq": lax.rem(zz, LINE) * 2 + cc,
        }

    def xat(d):
        return lax.rem(x + (SIDE + d) % SIDE, SIDE)

    def yat(d):
        return lax.rem(y + (SIDE + d) % SIDE, SIDE)

    partner = at(x, y, z, 1 - c)

    barrier = pltpu.get_barrier_semaphore()

    def greet(target):
        pl.semaphore_signal(barrier, inc=1, device_id=target, device_id_type=MESH)

    greet(partner)
    for d in range(1, SIDE):
        greet(at(xat(d), y, z, c))
        greet(at(x, yat(d), z, c))

    def greet_z(d, carry):
        greet(at(x, y, lax.rem(z + d, RING), c))
        return carry

    lax.fori_loop(1, RING, greet_z, 0)
    mine = pl.ds(pl.multiple_of(c * 128, 128), 128)
    theirs = pl.ds(pl.multiple_of((1 - c) * 128, 128), 128)
    tok_local = pltpu.make_async_copy(tokens, tok.at[mine], misc.at[0])
    tok_local.start()
    pl.semaphore_wait(barrier, 1 + 2 * (SIDE - 1) + RING - 1)

    def remote(src, dst, send, recv, target):
        return pltpu.make_async_remote_copy(
            src_ref=src, dst_ref=dst, send_sem=send, recv_sem=recv,
            device_id=target, device_id_type=MESH,
        )

    w_copy = remote(shard, other, misc.at[3], misc.at[4], partner)
    w_copy.start()
    tok_copy = remote(tokens, tok.at[mine], misc.at[1], misc.at[2], partner)
    tok_copy.start()
    w_copy.wait_recv()

    own_shard = shard[...].astype(jnp.float32)
    other_shard = other[...].astype(jnp.float32)
    low = jnp.where(c == 0, own_shard, other_shard)
    high = jnp.where(c == 0, other_shard, own_shard)
    blk[0] = low[:, :128].astype(jnp.bfloat16)
    blk[1] = jnp.concatenate([low[:, 128:], high[:, :64]], axis=1).astype(jnp.bfloat16)
    blk[2] = high[:, 64:].astype(jnp.bfloat16)

    def place(zhalf, column):
        rows = pl.ds(pl.multiple_of(xy * ROWS + zhalf * SUB, SUB), SUB)
        return W.at[rows, pl.ds(pl.multiple_of(column, BLK), BLK)]

    def spread(j, keys_or_values):
        b = zl * 3 + j
        past = b - HEADS
        if keys_or_values:
            local = 8 + lax.div(past, KV_HEADS) * 2 + lax.rem(past, 2)
            wanted = (b >= HEADS) & (lax.rem(lax.div(past, 2), 2) == c)
        else:
            local = lax.rem(b, 8)
            wanted = (b < HEADS) & (lax.div(b, 8) == c)

        @pl.when(wanted)
        def _():
            where = place(zh, local * BLK)
            sem = zrecv.at[local * 2 + zh]

            def one(d, carry):
                remote(
                    blk.at[j], where, zsend.at[j], sem, at(x, y, lax.rem(z + d, RING), c)
                ).start()
                return carry

            lax.fori_loop(1, RING, one, 0)
            pltpu.make_async_copy(blk.at[j], where, sem).start()

    def spread_done(j):
        b = zl * 3 + j
        past = b - HEADS
        wanted = ((b < HEADS) & (lax.div(b, 8) == c)) | (
            (b >= HEADS) & (lax.rem(lax.div(past, 2), 2) == c)
        )

        @pl.when(wanted)
        def _():
            ref = W.at[pl.ds(0, SUB * (RING - 1)), pl.ds(0, BLK)]
            pltpu.make_async_copy(ref, ref, zsend.at[j]).wait()

    def landed(first, count):
        for local in range(first, first + count):
            for half in range(2):
                ref = place(half, local * BLK)
                pltpu.make_async_copy(ref, ref, zrecv.at[local * 2 + half]).wait()

    def piece(g, xx, yy):
        first, width, _ = GROUPS[g]
        rows = pl.ds(pl.multiple_of((xx * SIDE + yy) * ROWS, ROWS), ROWS)
        return W.at[rows, pl.ds(first, width)]

    def stage_one(g):
        ref = piece(g, x, y)
        for d in range(1, SIDE):
            target = at(xat(d), y, z, c) if GROUPS[g][2] else at(x, yat(d), z, c)
            remote(ref, ref, s1send.at[g], s1recv.at[g * 3 + d - 1], target).start()

    def stage_two(g, d):
        ref = piece(g, xat(-d), y) if GROUPS[g][2] else piece(g, x, yat(-d))
        if d:
            pltpu.make_async_copy(ref, ref, s1recv.at[g * 3 + d - 1]).wait()
        for e in range(1, SIDE):
            target = at(x, yat(e), z, c) if GROUPS[g][2] else at(xat(e), y, z, c)
            remote(ref, ref, s2send.at[g], s2recv.at[g * 12 + d * 3 + e - 1], target).start()

    def gathered(g):
        for d in range(SIDE):
            for e in range(1, SIDE):
                if GROUPS[g][2]:
                    ref = piece(g, xat(-d), yat(-e))
                else:
                    ref = piece(g, xat(-e), yat(-d))
                pltpu.make_async_copy(ref, ref, s2recv.at[g * 12 + d * 3 + e - 1]).wait()

    def planes_done(g):
        first, width, _ = GROUPS[g]
        ref = W.at[pl.ds(0, 3 * ROWS), pl.ds(first, width)]
        pltpu.make_async_copy(ref, ref, s1send.at[g]).wait()
        ref = W.at[pl.ds(0, 12 * ROWS), pl.ds(first, width)]
        pltpu.make_async_copy(ref, ref, s2send.at[g]).wait()

    def rotated(value):
        return value * cos[...] + pltpu.roll(value, 64, 1) * sin[...]

    for j in range(3):
        spread(j, True)
    landed(8, 2)
    stage_one(0)
    landed(10, 2)
    stage_one(1)
    for j in range(3):
        spread(j, False)
    stage_two(0, 0)
    stage_two(1, 0)
    for d in range(1, SIDE):
        stage_two(0, d)
        stage_two(1, d)
    landed(0, 4)
    stage_one(2)
    landed(4, 4)
    stage_one(3)
    stage_two(2, 0)
    stage_two(3, 0)
    tok_local.wait()
    tok_copy.wait_recv()

    gathered(0)
    keys = jnp.dot(tok[...], W[:, 1024:1280], preferred_element_type=jnp.float32)
    for h in range(2):
        kv[zl, h] = rotated(keys[:, h * 128 : (h + 1) * 128]).astype(jnp.bfloat16)
    gathered(1)
    values = jnp.dot(tok[...], W[:, 1280:1536], preferred_element_type=jnp.float32)
    for h in range(2):
        kv[zl, 2 + h] = values[:, h * 128 : (h + 1) * 128].astype(jnp.bfloat16)

    def kv_copy(s):
        ref = kv.at[zl - s]
        return remote(ref, ref, kvsend.at[s], kvrecv.at[s], at(x, y, z + 1, c))

    @pl.when(zl < LINE - 1)
    def _():
        kv_copy(0).start()

    for d in range(1, SIDE):
        stage_two(2, d)
        stage_two(3, d)

    def arrive(s):
        @pl.when(zl > s)
        def _():
            ref = kv.at[zl - 1 - s]
            pltpu.make_async_copy(ref, ref, kvrecv.at[s]).wait()

        if s + 1 < LINE - 1:

            @pl.when((zl > s) & (zl < LINE - 1))
            def _():
                kv_copy(s + 1).start()

    def project_queries():
        def pair(i, carry):
            cols = pl.ds(pl.multiple_of(i * 256, 256), 256)
            two = jnp.dot(tok[...], W[:, cols], preferred_element_type=jnp.float32)
            q[i * 2] = rotated(two[:, :128]).astype(jnp.bfloat16)
            q[i * 2 + 1] = rotated(two[:, 128:]).astype(jnp.bfloat16)
            return carry

        lax.fori_loop(0, 4, pair, 0)

    NT = (((1,), (1,)), ((), ()))

    def diagonal():
        keep = lax.broadcasted_iota(jnp.int32, (256, 256), 0) >= lax.broadcasted_iota(
            jnp.int32, (256, 256), 1
        )

        def group(i, carry):
            key, value = kv[zl, i], kv[zl, 2 + i]
            for j in range(4):
                h = i * 4 + j
                s = lax.dot_general(q[h], key, NT, preferred_element_type=jnp.float32)
                s = jnp.where(keep, s, -jnp.inf)
                m = jnp.max(s, axis=-1, keepdims=True)
                p = jnp.exp((s - m) * SCALE)
                top[h] = m
                total[h] = jnp.sum(p, axis=-1, keepdims=True)
                acc[h] = jnp.dot(
                    p.astype(jnp.bfloat16), value, preferred_element_type=jnp.float32
                )
            return carry

        lax.fori_loop(0, 2, group, 0)

    def attend(step):
        @pl.when(zl > step)
        def _():
            slot = zl - 1 - step

            def group(i, carry):
                key, value = kv[slot, i], kv[slot, 2 + i]
                for j in range(4):
                    h = i * 4 + j
                    s = lax.dot_general(q[h], key, NT, preferred_element_type=jnp.float32)
                    old = top[h]
                    m = jnp.maximum(old, jnp.max(s, axis=-1, keepdims=True))
                    p = jnp.exp((s - m) * SCALE)
                    shrink = jnp.exp((old - m) * SCALE)
                    top[h] = m
                    total[h] = total[h] * shrink + jnp.sum(p, axis=-1, keepdims=True)
                    acc[h] = acc[h] * shrink + jnp.dot(
                        p.astype(jnp.bfloat16), value, preferred_element_type=jnp.float32
                    )
                return carry

            lax.fori_loop(0, 2, group, 0)

    for s in range(4):
        arrive(s)
    gathered(2)
    gathered(3)
    project_queries()
    diagonal()
    attend(0)
    arrive(4)
    attend(1)
    attend(2)
    arrive(5)
    attend(3)
    attend(4)
    arrive(6)
    attend(5)
    attend(6)

    for h in range(8):
        value = (acc[h] / total[h]).astype(jnp.bfloat16)
        ctx[:, h * 128 : (h + 1) * 128] = value
    columns = pl.ds(pl.multiple_of(c * 1024, 1024), 1024)
    out_copy = remote(
        ctx.at[theirs], out.at[:, columns], misc.at[6], misc.at[7], partner
    )
    out_copy.start()
    out_local = pltpu.make_async_copy(ctx.at[mine], out.at[:, columns], misc.at[5])
    out_local.start()

    w_copy.wait_send()
    tok_copy.wait_send()
    for j in range(3):
        spread_done(j)
    for g in range(4):
        planes_done(g)
    for s in range(LINE - 1):

        @pl.when((zl >= s) & (zl < LINE - 1))
        def _(s=s):
            kv_copy(s).wait_send()

    out_local.wait()
    out_copy.wait()


def shards(tokens, master, moment_one, moment_two, gradient):
    new_master = adam_step(master, moment_one, moment_two, gradient)
    weights = new_master.astype(jnp.bfloat16)
    half = HEAD_DIM // 2
    frequency = rope_theta ** (-(jnp.arange(half).astype(jnp.float32) * 2.0) / HEAD_DIM)
    chip = lax.div(lax.axis_index("seq"), 2)
    positions = (chip * 256 + jnp.arange(256)).astype(jnp.float32)
    angles = positions[:, None] * frequency[None, :]
    cosine, sine = jnp.cos(angles), jnp.sin(angles)
    cos = jnp.concatenate([cosine, cosine], axis=1)
    sin = jnp.concatenate([-sine, sine], axis=1)
    vmem = pl.BlockSpec(memory_space=pltpu.VMEM)
    anywhere = pl.BlockSpec(memory_space=pl.ANY)
    bf16, f32 = jnp.bfloat16, jnp.float32
    dma = pltpu.SemaphoreType.DMA
    context = pl.pallas_call(
        kernel,
        name="gather_attend",
        out_shape=jax.ShapeDtypeStruct((128, 2048), bf16),
        in_specs=[anywhere, vmem, vmem, vmem],
        out_specs=anywhere,
        scratch_shapes=[
            pltpu.VMEM((64, 192), bf16),
            pltpu.VMEM((3, 64, 128), bf16),
            pltpu.VMEM((2048, 1536), bf16),
            pltpu.VMEM((256, 2048), bf16),
            pltpu.VMEM((LINE, 4, 256, 128), bf16),
            pltpu.VMEM((8, 256, 128), bf16),
            pltpu.VMEM((8, 256, 128), f32),
            pltpu.VMEM((8, 256, 1), f32),
            pltpu.VMEM((8, 256, 1), f32),
            pltpu.VMEM((256, 1024), bf16),
            dma((8,)), dma((3,)), dma((24,)), dma((4,)), dma((12,)), dma((4,)), dma((48,)),
            dma((7,)), dma((7,)),
        ],
        compiler_params=pltpu.CompilerParams(
            collective_id=0, has_side_effects=True, vmem_limit_bytes=48 * 1024 * 1024
        ),
    )(tokens[0], weights, cos, sin)
    return context[None], new_master


def solution(mesh):
    placed = (P("dp", "seq", None), P("dp", "seq"), P("dp", "seq"), P("dp", "seq"), P("dp", "seq"))
    return jax.shard_map(
        shards,
        mesh=mesh,
        in_specs=placed,
        out_specs=(P("dp", "seq", None), P("dp", "seq")),
        check_vma=False,
    )
```

time: 545 us -> 120 us (0.22)
  the two profiles are of different devices: /device:TPU:1 before, /device:TPU:497 now
where the time goes in v1:
time: 120 us
  Pallas kernels  116 us (97%)
  other arithmetic  2.31 us (2%)
    pallas_call x1, Pallas kernels, shards(): pl.pallas_call(kernel, name='gather_attend', out_shape=jax.ShapeDtypeStru...  116 us

profile of v1, /device:TPU:497, one launch (start us, length us, event | category | flops | bytes accessed | tf_op | source)
XLA Modules:
  0.0 120.3 jit_solution(16215503735977372955)
XLA Ops:
  0.7 1.6 %fusion.7 = (bf16[64,192]{1,0:T(8,128)(2,1)S(1)}, f32[64,192]{1,0:T(8,128)}) fusion(f32[64,192]{1,0:T(8,128)} %param.6, f32[64,192]{1,0:T(8,128)} %param.9, f32[64,192]{1,0:T(8,128)} %param.8, f32[64,192]{1,0:T(8,128)} %param.7), kind=kLoop, calls=%fused_computation.15 | loop fusion | flops 184320 | bytes 270336 | tf_op jit(solution)/shard_map/convert_element_type | solution.py:352
  2.3 0.0 copy-start
  2.3 0.5 fusion.6
  2.8 0.1 pad_maximum_fusion
  3.0 0.4 copy-done
  3.3 116.1 %gather_attend.1 = bf16[128,2048]{1,0:T(8,128)(2,1)S(1)} custom-call(bf16[128,2048]{1,0:T(8,128)(2,1)S(1)} %bitcast.3, bf16[64,192]{1,0:T(8,128)(2,1)S(1)} %get-tuple-element.2.shard, f32[256,128]{1,0:T(8,128)S(1)} %get-tuple-element.7.cos, f32[256,128]{1,0:T(8,128)S(1)} %get-tuple-element.8.sin), custom_call_target="tpu_custom_call" | custom-call | tf_op jit(solution)/shard_map/gather_attend/pallas_call | solution.py:365
  119.5 0.8 copy.8
  (2 shorter events, 0.0 us)
Async XLA Ops:
  2.3 1.0 copy-start

commit v2 on v1

v2 whole, which is shorter than its diff:
```python
import functools
import math

import jax
import jax.numpy as jnp
from jax import lax
from jax.experimental import pallas as pl
from jax.experimental.pallas import tpu as pltpu
from jax.sharding import PartitionSpec as P

HEADS = 16
KV_HEADS = 4
HEAD_DIM = 128
SIDE = 4
LINE = 8
RING = 16
MESH = pl.DeviceIdType.MESH

beta_one = 0.9
beta_two = 0.999
learn_rate = 0.005
decay_rate = 0.1
adam_eps = 1e-08
rope_theta = 500000.0
correct_one = 1.0 - math.exp(1000.0 * math.log(beta_one))
correct_two = 1.0 - math.exp(1000.0 * math.log(beta_two))

SCALE = 1.0 / math.sqrt(HEAD_DIM)
BLK = 128
SUB = 64
ROWS = 128
GROUPS = (
    (1024, 128, True), (1152, 128, False), (1280, 128, True), (1408, 128, False),
    (0, 256, True), (512, 256, False), (256, 256, True), (768, 256, False),
)
COARSE = (8, 4, 12)
FINE = (1, 15, 2)
POWER = SCALE / math.log(2.0)


def adam_step(master, moment_one, moment_two, gradient):
    first = beta_one * moment_one + (1.0 - beta_one) * gradient
    second = beta_two * moment_two + (1.0 - beta_two) * gradient * gradient
    update = first / correct_one / (jnp.sqrt(second / correct_two) + adam_eps)
    return master - learn_rate * (update + decay_rate * master)


def kernel(
    tokens, shard, cos, sin, out,
    other, blk, W, tok, keys, values, q, acc, top, total, ctx,
    misc, zsend, zpass, zrecv, s1send, s1recv, s2send, s2recv, kvsend, kvrecv,
):
    dp, seq = lax.axis_index("dp"), lax.axis_index("seq")
    zh = lax.rem(dp, 2)
    xy = lax.div(dp, 2)
    x, y = lax.div(xy, SIDE), lax.rem(xy, SIDE)
    c = lax.rem(seq, 2)
    zl = lax.div(seq, 2)
    z = zh * LINE + zl

    def at(xx, yy, zz, cc):
        return {
            "dp": (xx * SIDE + yy) * 2 + lax.div(zz, LINE),
            "seq": lax.rem(zz, LINE) * 2 + cc,
        }

    def xat(d):
        return lax.rem(x + (SIDE + d) % SIDE, SIDE)

    def yat(d):
        return lax.rem(y + (SIDE + d) % SIDE, SIDE)

    partner = at(x, y, z, 1 - c)

    barrier = pltpu.get_barrier_semaphore()

    def greet(target):
        pl.semaphore_signal(barrier, inc=1, device_id=target, device_id_type=MESH)

    greet(partner)
    for d in range(1, SIDE):
        greet(at(xat(d), y, z, c))
        greet(at(x, yat(d), z, c))

    def greet_z(d, carry):
        greet(at(x, y, lax.rem(z + d, RING), c))
        return carry

    lax.fori_loop(1, RING, greet_z, 0)
    mine = pl.ds(pl.multiple_of(c * 128, 128), 128)
    theirs = pl.ds(pl.multiple_of((1 - c) * 128, 128), 128)
    tok_local = pltpu.make_async_copy(tokens, tok.at[mine], misc.at[0])
    tok_local.start()
    pl.semaphore_wait(barrier, 1 + 2 * (SIDE - 1) + RING - 1)

    def remote(src, dst, send, recv, target):
        return pltpu.make_async_remote_copy(
            src_ref=src, dst_ref=dst, send_sem=send, recv_sem=recv,
            device_id=target, device_id_type=MESH,
        )

    w_copy = remote(shard, other, misc.at[3], misc.at[4], partner)
    w_copy.start()
    tok_copy = remote(tokens, tok.at[mine], misc.at[1], misc.at[2], partner)
    tok_copy.start()
    w_copy.wait_recv()

    own_shard = shard[...].astype(jnp.float32)
    other_shard = other[...].astype(jnp.float32)
    low = jnp.where(c == 0, own_shard, other_shard)
    high = jnp.where(c == 0, other_shard, own_shard)
    blk[0] = low[:, :128].astype(jnp.bfloat16)
    blk[1] = jnp.concatenate([low[:, 128:], high[:, :64]], axis=1).astype(jnp.bfloat16)
    blk[2] = high[:, 64:].astype(jnp.bfloat16)

    def place(zhalf, column):
        rows = pl.ds(pl.multiple_of(xy * ROWS + zhalf * SUB, SUB), SUB)
        return W.at[rows, pl.ds(pl.multiple_of(column, BLK), BLK)]

    def block_of(line, j, keys_or_values):
        b = line * 3 + j
        past = b - HEADS
        if keys_or_values:
            local = 8 + lax.div(past, KV_HEADS) * 2 + lax.rem(past, 2)
            return local, (b >= HEADS) & (lax.rem(lax.div(past, 2), 2) == c)
        return lax.rem(b, 8), (b < HEADS) & (lax.div(b, 8) == c)

    def z_send(src, where, send, recv, steps):
        for d in steps:
            remote(src, where, send, recv, at(x, y, lax.rem(z + d, RING), c)).start()

    def spread(kind):
        for j in range(3):
            local, wanted = block_of(zl, j, kind)

            @pl.when(wanted)
            def _(j=j, local=local):
                where = place(zh, local * BLK)
                sem = zrecv.at[local * 2 + zh]
                z_send(blk.at[j], where, zsend.at[j], sem, COARSE + FINE)
                pltpu.make_async_copy(blk.at[j], where, sem).start()

    def pass_on(kind):
        for i, d in enumerate(COARSE):
            source = lax.rem(z + RING - d, RING)
            half = lax.div(source, LINE)
            for j in range(3):
                local, wanted = block_of(lax.rem(source, LINE), j, kind)

                @pl.when(wanted)
                def _(i=i, j=j, local=local, half=half):
                    where = place(half, local * BLK)
                    sem = zrecv.at[local * 2 + half]
                    pltpu.make_async_copy(where, where, sem).wait()
                    z_send(where, where, zpass.at[i * 3 + j], sem, FINE)

    def spread_done():
        for kind in (True, False):
            for j in range(3):
                _, wanted = block_of(zl, j, kind)

                @pl.when(wanted)
                def _(j=j):
                    ref = W.at[pl.ds(0, SUB * 6), pl.ds(0, BLK)]
                    pltpu.make_async_copy(ref, ref, zsend.at[j]).wait()

                for i, d in enumerate(COARSE):
                    _, passed = block_of(lax.rem(z + RING - d, LINE), j, kind)

                    @pl.when(passed)
                    def _(i=i, j=j):
                        ref = W.at[pl.ds(0, SUB * 3), pl.ds(0, BLK)]
                        pltpu.make_async_copy(ref, ref, zpass.at[i * 3 + j]).wait()

    def landed(first, count):
        for local in range(first, first + count):
            if local < 8:
                b = c * 8 + local
            elif local < 10:
                b = HEADS + c * 2 + local - 8
            else:
                b = HEADS + KV_HEADS + c * 2 + local - 10
            for half in range(2):
                steps = lax.rem(z + RING - (lax.div(b, 3) + half * LINE), RING)

                @pl.when((lax.rem(steps, 4) != 0) | (steps == 0))
                def _(local=local, half=half):
                    ref = place(half, local * BLK)
                    pltpu.make_async_copy(ref, ref, zrecv.at[local * 2 + half]).wait()

    def piece(g, xx, yy):
        first, width, _ = GROUPS[g]
        rows = pl.ds(pl.multiple_of((xx * SIDE + yy) * ROWS, ROWS), ROWS)
        return W.at[rows, pl.ds(first, width)]

    def stage_one(g):
        ref = piece(g, x, y)
        for d in range(1, SIDE):
            target = at(xat(d), y, z, c) if GROUPS[g][2] else at(x, yat(d), z, c)
            remote(ref, ref, s1send.at[g], s1recv.at[g * 3 + d - 1], target).start()

    def stage_two(g, d):
        ref = piece(g, xat(-d), y) if GROUPS[g][2] else piece(g, x, yat(-d))
        if d:
            pltpu.make_async_copy(ref, ref, s1recv.at[g * 3 + d - 1]).wait()
        for e in range(1, SIDE):
            target = at(x, yat(e), z, c) if GROUPS[g][2] else at(xat(e), y, z, c)
            remote(ref, ref, s2send.at[g], s2recv.at[g * 12 + d * 3 + e - 1], target).start()

    def gathered(g):
        for d in range(SIDE):
            for e in range(1, SIDE):
                if GROUPS[g][2]:
                    ref = piece(g, xat(-d), yat(-e))
                else:
                    ref = piece(g, xat(-e), yat(-d))
                pltpu.make_async_copy(ref, ref, s2recv.at[g * 12 + d * 3 + e - 1]).wait()

    def planes_done(g):
        first, width, _ = GROUPS[g]
        ref = W.at[pl.ds(0, 3 * ROWS), pl.ds(first, width)]
        pltpu.make_async_copy(ref, ref, s1send.at[g]).wait()
        ref = W.at[pl.ds(0, 12 * ROWS), pl.ds(first, width)]
        pltpu.make_async_copy(ref, ref, s2send.at[g]).wait()

    def rotated(value):
        return value * cos[...] + pltpu.roll(value, 64, 1) * sin[...]

    def kv_copy(kind, s):
        ref = (values if kind else keys).at[zl - s]
        sem = kind * (LINE - 1) + s
        return remote(ref, ref, kvsend.at[sem], kvrecv.at[sem], at(x, y, z + 1, c))

    def send_own(kind):
        @pl.when(zl < LINE - 1)
        def _():
            kv_copy(kind, 0).start()

    def arrive(kind, s):
        @pl.when(zl > s)
        def _():
            ref = (values if kind else keys).at[zl - 1 - s]
            pltpu.make_async_copy(ref, ref, kvrecv.at[kind * (LINE - 1) + s]).wait()

        if s + 1 < LINE - 1:

            @pl.when((zl > s) & (zl < LINE - 1))
            def _():
                kv_copy(kind, s + 1).start()

    def project_queries(offset):
        def pair(i, carry):
            cols = pl.ds(pl.multiple_of(i * 512 + offset * 128, 256), 256)
            two = jnp.dot(tok[...], W[:, cols], preferred_element_type=jnp.float32)
            for j in range(2):
                one = rotated(two[:, j * 128 : (j + 1) * 128])
                q[i * 4 + offset + j] = one.T.astype(jnp.bfloat16)
            return carry

        lax.fori_loop(0, 2, pair, 0)

    def attend(slot, offset, masked):
        def group(i, carry):
            key, value = keys[slot, i], values[slot, i]
            for j in range(2):
                h = i * 4 + offset + j
                s = jnp.dot(key, q[h], preferred_element_type=jnp.float32)
                if masked:
                    row = lax.broadcasted_iota(jnp.int32, (256, 256), 0)
                    column = lax.broadcasted_iota(jnp.int32, (256, 256), 1)
                    s = jnp.where(row <= column, s, -jnp.inf)
                    m = jnp.max(s, axis=0, keepdims=True)
                else:
                    old = top[h]
                    m = jnp.maximum(old, jnp.max(s, axis=0, keepdims=True))
                p = jnp.exp2((s - m) * POWER)
                mass = jnp.sum(p, axis=0, keepdims=True)
                part = jnp.dot(value, p.astype(jnp.bfloat16), preferred_element_type=jnp.float32)
                top[h] = m
                if masked:
                    total[h] = mass
                    acc[h] = part
                else:
                    shrink = jnp.exp2((old - m) * POWER)
                    total[h] = total[h] * shrink + mass
                    acc[h] = acc[h] * shrink + part
            return carry

        lax.fori_loop(0, 2, group, 0)

    def attend_steps(offset, steps):
        for s in steps:

            @pl.when(zl > s)
            def _(s=s):
                attend(zl - 1 - s, offset, False)

    spread(True)
    pass_on(True)
    spread(False)
    landed(8, 1)
    stage_one(0)
    landed(9, 1)
    stage_one(1)
    landed(10, 1)
    stage_one(2)
    landed(11, 1)
    stage_one(3)
    stage_two(0, 0)
    stage_two(1, 0)
    for d in range(1, SIDE):
        stage_two(0, d)
        stage_two(1, d)
    stage_two(2, 0)
    stage_two(3, 0)
    for d in range(1, SIDE):
        stage_two(2, d)
        stage_two(3, d)
    pass_on(False)
    tok_local.wait()
    tok_copy.wait_recv()
    gathered(0)
    gathered(1)
    two = jnp.dot(tok[...], W[:, 1024:1280], preferred_element_type=jnp.float32)
    for h in range(2):
        keys[zl, h] = rotated(two[:, h * 128 : (h + 1) * 128]).astype(jnp.bfloat16)
    send_own(0)
    landed(0, 2)
    stage_one(4)
    landed(4, 2)
    stage_one(5)
    stage_two(4, 0)
    stage_two(5, 0)
    gathered(2)
    gathered(3)
    two = jnp.dot(tok[...], W[:, 1280:1536], preferred_element_type=jnp.float32)
    for h in range(2):
        values[zl, h] = two[:, h * 128 : (h + 1) * 128].T.astype(jnp.bfloat16)
    send_own(1)
    landed(2, 2)
    stage_one(6)
    landed(6, 2)
    stage_one(7)
    arrive(0, 0)
    arrive(1, 0)
    for d in range(1, SIDE):
        stage_two(4, d)
        stage_two(5, d)
    stage_two(6, 0)
    stage_two(7, 0)
    arrive(0, 1)
    arrive(1, 1)
    for d in range(1, SIDE):
        stage_two(6, d)
        stage_two(7, d)
    arrive(0, 2)
    arrive(1, 2)
    arrive(0, 3)
    gathered(4)
    gathered(5)
    arrive(1, 3)
    project_queries(0)
    attend(zl, 0, True)
    attend_steps(0, (0, 1))
    arrive(0, 4)
    attend_steps(0, (2, 3))
    arrive(1, 4)
    attend_steps(0, (4,))
    arrive(0, 5)
    arrive(1, 5)
    gathered(6)
    gathered(7)
    project_queries(2)
    attend(zl, 2, True)
    attend_steps(2, (0, 1, 2, 3))
    arrive(0, 6)
    attend_steps(2, (4, 5))
    attend_steps(0, (5,))
    arrive(1, 6)
    attend_steps(2, (6,))
    attend_steps(0, (6,))

    for h in range(8):
        value = acc[h] * (1.0 / total[h])
        ctx[:, h * 128 : (h + 1) * 128] = value.T.astype(jnp.bfloat16)
    columns = pl.ds(pl.multiple_of(c * 1024, 1024), 1024)
    out_copy = remote(
        ctx.at[theirs], out.at[:, columns], misc.at[6], misc.at[7], partner
    )
    out_copy.start()
    out_local = pltpu.make_async_copy(ctx.at[mine], out.at[:, columns], misc.at[5])
    out_local.start()

    w_copy.wait_send()
    tok_copy.wait_send()
    spread_done()
    for g in range(len(GROUPS)):
        planes_done(g)
    for kind in range(2):
        for s in range(LINE - 1):

            @pl.when((zl >= s) & (zl < LINE - 1))
            def _(kind=kind, s=s):
                kv_copy(kind, s).wait_send()

    out_local.wait()
    out_copy.wait()


def shards(tokens, master, moment_one, moment_two, gradient):
    new_master = adam_step(master, moment_one, moment_two, gradient)
    weights = new_master.astype(jnp.bfloat16)
    half = HEAD_DIM // 2
    frequency = rope_theta ** (-(jnp.arange(half).astype(jnp.float32) * 2.0) / HEAD_DIM)
    chip = lax.div(lax.axis_index("seq"), 2)
    positions = (chip * 256 + jnp.arange(256)).astype(jnp.float32)
    angles = positions[:, None] * frequency[None, :]
    cosine, sine = jnp.cos(angles), jnp.sin(angles)
    cos = jnp.concatenate([cosine, cosine], axis=1)
    sin = jnp.concatenate([-sine, sine], axis=1)
    vmem = pl.BlockSpec(memory_space=pltpu.VMEM)
    anywhere = pl.BlockSpec(memory_space=pl.ANY)
    bf16, f32 = jnp.bfloat16, jnp.float32
    dma = pltpu.SemaphoreType.DMA
    context = pl.pallas_call(
        kernel,
        name="gather_attend",
        out_shape=jax.ShapeDtypeStruct((128, 2048), bf16),
        in_specs=[anywhere, vmem, vmem, vmem],
        out_specs=anywhere,
        scratch_shapes=[
            pltpu.VMEM((64, 192), bf16),
            pltpu.VMEM((3, 64, 128), bf16),
            pltpu.VMEM((2048, 1536), bf16),
            pltpu.VMEM((256, 2048), bf16),
            pltpu.VMEM((LINE, 2, 256, 128), bf16),
            pltpu.VMEM((LINE, 2, 128, 256), bf16),
            pltpu.VMEM((8, 128, 256), bf16),
            pltpu.VMEM((8, 128, 256), f32),
            pltpu.VMEM((8, 1, 256), f32),
            pltpu.VMEM((8, 1, 256), f32),
            pltpu.VMEM((256, 1024), bf16),
            dma((8,)), dma((3,)), dma((9,)), dma((24,)), dma((8,)), dma((24,)), dma((8,)),
            dma((96,)), dma((14,)), dma((14,)),
        ],
        compiler_params=pltpu.CompilerParams(
            collective_id=0, has_side_effects=True, vmem_limit_bytes=48 * 1024 * 1024
        ),
    )(tokens[0], weights, cos, sin)
    return context[None], new_master


def solution(mesh):
    placed = (P("dp", "seq", None), P("dp", "seq"), P("dp", "seq"), P("dp", "seq"), P("dp", "seq"))
    return jax.shard_map(
        shards,
        mesh=mesh,
        in_specs=placed,
        out_specs=(P("dp", "seq", None), P("dp", "seq")),
        check_vma=False,
    )
```

time: 120 us -> 96.9 us (0.81)
  the two profiles are of different devices: /device:TPU:497 before, /device:TPU:225 now
where the time goes in v2:
time: 96.9 us; the launch traced here: 96.7 us
  Pallas kernels  92.5 us (95%)
  other arithmetic  2.31 us (2%)
  local copies, waits for them, and re-layouts  1.16 us (1%)
    pallas_call x1, Pallas kernels, shards(): pl.pallas_call(kernel, name='gather_attend', out_shape=jax.ShapeDtypeStru...  92.5 us

profile of v2, /device:TPU:225, one launch (start us, length us, event | category | flops | bytes accessed | tf_op | source)
XLA Modules:
  0.0 96.7 jit_solution(2241889740319191171)
XLA Ops:
  0.7 1.6 %fusion.7 = (bf16[64,192]{1,0:T(8,128)(2,1)S(1)}, f32[64,192]{1,0:T(8,128)}) fusion(f32[64,192]{1,0:T(8,128)} %param.6, f32[64,192]{1,0:T(8,128)} %param.9, f32[64,192]{1,0:T(8,128)} %param.8, f32[64,192]{1,0:T(8,128)} %param.7), kind=kLoop, calls=%fused_computation.15 | loop fusion | flops 184320 | bytes 270336 | tf_op jit(solution)/shard_map/convert_element_type | solution.py:412
  2.3 0.0 copy-start
  2.3 0.5 fusion.6
  2.8 0.1 pad_maximum_fusion
  3.0 0.4 copy-done
  3.3 92.5 %gather_attend.1 = bf16[128,2048]{1,0:T(8,128)(2,1)S(1)} custom-call(bf16[128,2048]{1,0:T(8,128)(2,1)S(1)} %bitcast.3, bf16[64,192]{1,0:T(8,128)(2,1)S(1)} %get-tuple-element.2.shard, f32[256,128]{1,0:T(8,128)S(1)} %get-tuple-element.7.cos, f32[256,128]{1,0:T(8,128)S(1)} %get-tuple-element.8.sin), custom_call_target="tpu_custom_call" | custom-call | tf_op jit(solution)/shard_map/gather_attend/pallas_call | solution.py:425
  95.9 0.8 copy.8
  (2 shorter events, 0.0 us)
Async XLA Ops:
  2.3 1.0 %copy-start = (bf16[1,128,2048]{2,1,0:T(8,128)(2,1)S(1)}, bf16[1,128,2048]{2,1,0:T(8,128)(2,1)}, u32[]{:S(2)}) copy-start(bf16[1,128,2048]{2,1,0:T(8,128)(2,1)} %param.5) | copy-start | bytes 1572868

commit v3 on v2

--- a/solution.py
+++ b/solution.py
@@ -35,6 +35,7 @@
 )
 COARSE = (8, 4, 12)
 FINE = (1, 15, 2)
+STEPS = 5
 POWER = SCALE / math.log(2.0)
 
 
@@ -47,8 +48,8 @@
 
 def kernel(
     tokens, shard, cos, sin, out,
-    other, blk, W, tok, keys, values, q, acc, top, total, ctx,
-    misc, zsend, zpass, zrecv, s1send, s1recv, s2send, s2recv, kvsend, kvrecv,
+    other, blk, W, tok, prev, keys, values, q, acc, top, total, ctx,
+    far_keys, far_values, misc, zsend, zpass, zrecv, s1send, s1recv, s2send, s2recv, kvsend, kvrecv, wrapsend, wraprecv,
 ):
     dp, seq = lax.axis_index("dp"), lax.axis_index("seq")
     zh = lax.rem(dp, 2)
@@ -188,33 +189,67 @@
                     ref = place(half, local * BLK)
                     pltpu.make_async_copy(ref, ref, zrecv.at[local * 2 + half]).wait()
 
-    def piece(g, xx, yy):
-        first, width, _ = GROUPS[g]
-        rows = pl.ds(pl.multiple_of((xx * SIDE + yy) * ROWS, ROWS), ROWS)
-        return W.at[rows, pl.ds(first, width)]
-
-    def stage_one(g):
-        ref = piece(g, x, y)
-        for d in range(1, SIDE):
-            target = at(xat(d), y, z, c) if GROUPS[g][2] else at(x, yat(d), z, c)
-            remote(ref, ref, s1send.at[g], s1recv.at[g * 3 + d - 1], target).start()
-
-    def stage_two(g, d):
-        ref = piece(g, xat(-d), y) if GROUPS[g][2] else piece(g, x, yat(-d))
-        if d:
-            pltpu.make_async_copy(ref, ref, s1recv.at[g * 3 + d - 1]).wait()
-        for e in range(1, SIDE):
-            target = at(x, yat(e), z, c) if GROUPS[g][2] else at(xat(e), y, z, c)
-            remote(ref, ref, s2send.at[g], s2recv.at[g * 12 + d * 3 + e - 1], target).start()
-
-    def gathered(g):
-        for d in range(SIDE):
-            for e in range(1, SIDE):
-                if GROUPS[g][2]:
-                    ref = piece(g, xat(-d), yat(-e))
-                else:
-                    ref = piece(g, xat(-e), yat(-d))
-                pltpu.make_async_copy(ref, ref, s2recv.at[g * 12 + d * 3 + e - 1]).wait()
+    def ring(g, stage, d):
+        along_x = GROUPS[g][2] == (stage == 1)
+
+        def ref(step, first=0, count=ROWS):
+            dx, dy = (-step, -d) if along_x else (-d, -step)
+            rows = pl.multiple_of((xat(dx) * SIDE + yat(dy)) * ROWS + first, SUB)
+            return W.at[pl.ds(rows, count), pl.ds(GROUPS[g][0], GROUPS[g][1])]
+
+        up = at(xat(1), y, z, c) if along_x else at(x, yat(1), z, c)
+        down = at(xat(-1), y, z, c) if along_x else at(x, yat(-1), z, c)
+        if stage == 1:
+            return ref, up, down, s1send.at[g], lambda i: s1recv.at[g * 4 + i]
+        return ref, up, down, s2send.at[g], lambda i: s2recv.at[(g * 4 + d) * 4 + i]
+
+    def begin(g, stage, d=0):
+        ref, up, down, send, recv = ring(g, stage, d)
+        remote(ref(0), ref(0), send, recv(0), up).start()
+        remote(ref(0), ref(0), send, recv(1), down).start()
+
+    def hand_on(g, stage, d=0):
+        ref, up, down, send, recv = ring(g, stage, d)
+        pltpu.make_async_copy(ref(1), ref(1), recv(0)).wait()
+        half = ref(1, 0, SUB)
+        remote(half, half, send, recv(2), up).start()
+        pltpu.make_async_copy(ref(3), ref(3), recv(1)).wait()
+        half = ref(3, SUB, SUB)
+        remote(half, half, send, recv(3), down).start()
+
+    def complete(g, stage, d=0):
+        ref, _, _, _, recv = ring(g, stage, d)
+        for i in range(2):
+            half = ref(2, i * SUB, SUB)
+            pltpu.make_async_copy(half, half, recv(2 + i)).wait()
+
+    def first_own(*groups):
+        for g in groups:
+            begin(g, 1)
+
+    def second_own(*groups):
+        for g in groups:
+            begin(g, 2, 0)
+
+    def first_near(*groups):
+        for g in groups:
+            hand_on(g, 1)
+            begin(g, 2, 1)
+            begin(g, 2, 3)
+
+    def first_far(*groups):
+        for g in groups:
+            complete(g, 1)
+            begin(g, 2, 2)
+
+    def second_near(d, *groups):
+        for g in groups:
+            hand_on(g, 2, d)
+
+    def gathered(*groups):
+        for g in groups:
+            for d in (0, 1, 3, 2):
+                complete(g, 2, d)
 
     def planes_done(g):
         first, width, _ = GROUPS[g]
@@ -223,37 +258,132 @@
         ref = W.at[pl.ds(0, 12 * ROWS), pl.ds(first, width)]
         pltpu.make_async_copy(ref, ref, s2send.at[g]).wait()
 
-    def rotated(value):
-        return value * cos[...] + pltpu.roll(value, 64, 1) * sin[...]
+    def rotated(value, first):
+        rows = slice(first, first + 256)
+        return value * cos[rows] + pltpu.roll(value, 64, 1) * sin[rows]
 
     def kv_copy(kind, s):
-        ref = (values if kind else keys).at[zl - s]
-        sem = kind * (LINE - 1) + s
+        ref = (values if kind else keys).at[zl - 1 - s]
+        sem = kind * STEPS + s
         return remote(ref, ref, kvsend.at[sem], kvrecv.at[sem], at(x, y, z + 1, c))
 
-    def send_own(kind):
-        @pl.when(zl < LINE - 1)
+    def wrap_out(kind):
+        return remote(
+            (values if kind else keys).at[0], far_values if kind else far_keys,
+            wrapsend.at[kind], wraprecv.at[kind], at(x, y, lax.rem(z + 9, RING), c),
+        )
+
+    def wrap_relay(kind):
+        return remote(
+            far_values if kind else far_keys, (values if kind else keys).at[0],
+            wrapsend.at[2 + kind], wraprecv.at[2 + kind], at(x, y, lax.rem(z + RING - 2, RING), c),
+        )
+
+    def relay(kind):
+        @pl.when(zl == 1)
+        def _():
+            ref = far_values if kind else far_keys
+            pltpu.make_async_copy(ref, ref, wraprecv.at[kind]).wait()
+            wrap_relay(kind).start()
+
+    def wrapped(kind):
+        @pl.when(zl == LINE - 1)
+        def _():
+            ref = (values if kind else keys).at[0]
+            pltpu.make_async_copy(ref, ref, wraprecv.at[2 + kind]).wait()
+
+    def attend_wrapped(offset):
+        @pl.when(zl == LINE - 1)
+        def _():
+            attend(0, offset, False)
+
+    def wrap_done():
+        for kind in range(2):
+
+            @pl.when(zl == 0)
+            def _(kind=kind):
+                wrap_out(kind).wait_send()
+
+            @pl.when(zl == 1)
+            def _(kind=kind):
+                wrap_relay(kind).wait_send()
+
+    def wrap_own(kind):
+        @pl.when(zl == 0)
+        def _():
+            wrap_out(kind).start()
+
+    def send_before(kind):
+        @pl.when((zl > 0) & (zl < LINE - 1))
         def _():
             kv_copy(kind, 0).start()
 
     def arrive(kind, s):
-        @pl.when(zl > s)
-        def _():
-            ref = (values if kind else keys).at[zl - 1 - s]
-            pltpu.make_async_copy(ref, ref, kvrecv.at[kind * (LINE - 1) + s]).wait()
-
-        if s + 1 < LINE - 1:
-
-            @pl.when((zl > s) & (zl < LINE - 1))
+        @pl.when(zl > s + 1)
+        def _():
+            ref = (values if kind else keys).at[zl - 2 - s]
+            pltpu.make_async_copy(ref, ref, kvrecv.at[kind * STEPS + s]).wait()
+
+        if s + 1 < STEPS:
+
+            @pl.when((zl > s + 1) & (zl < LINE - 1))
             def _():
                 kv_copy(kind, s + 1).start()
+
+    prev_copy = remote(tokens, prev.at[mine], misc.at[8], misc.at[9], at(x, y, z + 1, c))
+    prev_share = remote(prev.at[mine], prev.at[mine], misc.at[10], misc.at[11], partner)
+
+    def send_tokens():
+        @pl.when(zl < LINE - 1)
+        def _():
+            prev_copy.start()
+
+    def share_tokens():
+        @pl.when(zl > 0)
+        def _():
+            prev_copy.wait_recv()
+            prev_share.start()
+
+    def tokens_before():
+        @pl.when(zl > 0)
+        def _():
+            prev_share.wait_recv()
+
+    def make_keys(rows, slot, first):
+        two = jnp.dot(rows[...], W[:, 1024:1280], preferred_element_type=jnp.float32)
+        for h in range(2):
+            value = rotated(two[:, h * 128 : (h + 1) * 128], first)
+            keys[slot, h] = value.astype(jnp.bfloat16)
+
+    def make_values(rows, slot):
+        two = jnp.dot(rows[...], W[:, 1280:1536], preferred_element_type=jnp.float32)
+        for h in range(2):
+            values[slot, h] = two[:, h * 128 : (h + 1) * 128].T.astype(jnp.bfloat16)
+
+    def keys_of_both():
+        @pl.when(zl > 0)
+        def _():
+            make_keys(prev, zl - 1, 0)
+
+        send_before(0)
+        make_keys(tok, zl, 256)
+        wrap_own(0)
+
+    def values_of_both():
+        @pl.when(zl > 0)
+        def _():
+            make_values(prev, zl - 1)
+
+        send_before(1)
+        make_values(tok, zl)
+        wrap_own(1)
 
     def project_queries(offset):
         def pair(i, carry):
             cols = pl.ds(pl.multiple_of(i * 512 + offset * 128, 256), 256)
             two = jnp.dot(tok[...], W[:, cols], preferred_element_type=jnp.float32)
             for j in range(2):
-                one = rotated(two[:, j * 128 : (j + 1) * 128])
+                one = rotated(two[:, j * 128 : (j + 1) * 128], 256)
                 q[i * 4 + offset + j] = one.T.astype(jnp.bfloat16)
             return carry
 
@@ -288,97 +418,102 @@
 
         lax.fori_loop(0, 2, group, 0)
 
+    def attend_near(offset):
+        attend(zl, offset, True)
+
+        @pl.when(zl > 0)
+        def _():
+            attend(zl - 1, offset, False)
+
     def attend_steps(offset, steps):
         for s in steps:
 
-            @pl.when(zl > s)
+            @pl.when(zl > s + 1)
             def _(s=s):
-                attend(zl - 1 - s, offset, False)
+                attend(zl - 2 - s, offset, False)
 
     spread(True)
+    spread(False)
     pass_on(True)
-    spread(False)
-    landed(8, 1)
-    stage_one(0)
-    landed(9, 1)
-    stage_one(1)
-    landed(10, 1)
-    stage_one(2)
-    landed(11, 1)
-    stage_one(3)
-    stage_two(0, 0)
-    stage_two(1, 0)
-    for d in range(1, SIDE):
-        stage_two(0, d)
-        stage_two(1, d)
-    stage_two(2, 0)
-    stage_two(3, 0)
-    for d in range(1, SIDE):
-        stage_two(2, d)
-        stage_two(3, d)
     pass_on(False)
+    send_tokens()
+    for g in range(4):
+        landed(8 + g, 1)
+        first_own(g)
+    second_own(0, 1)
+    first_near(0, 1)
+    second_own(2, 3)
+    second_near(0, 0, 1)
+    first_near(2, 3)
+    first_far(0, 1)
+    second_near(1, 0, 1)
+    second_near(3, 0, 1)
+    second_near(0, 2, 3)
+    first_far(2, 3)
+    landed(0, 2)
+    first_own(4)
+    landed(4, 2)
+    first_own(5)
+    second_near(2, 0, 1)
+    second_near(1, 2, 3)
+    second_near(3, 2, 3)
+    second_own(4, 5)
     tok_local.wait()
     tok_copy.wait_recv()
-    gathered(0)
-    gathered(1)
-    two = jnp.dot(tok[...], W[:, 1024:1280], preferred_element_type=jnp.float32)
-    for h in range(2):
-        keys[zl, h] = rotated(two[:, h * 128 : (h + 1) * 128]).astype(jnp.bfloat16)
-    send_own(0)
-    landed(0, 2)
-    stage_one(4)
-    landed(4, 2)
-    stage_one(5)
-    stage_two(4, 0)
-    stage_two(5, 0)
-    gathered(2)
-    gathered(3)
-    two = jnp.dot(tok[...], W[:, 1280:1536], preferred_element_type=jnp.float32)
-    for h in range(2):
-        values[zl, h] = two[:, h * 128 : (h + 1) * 128].T.astype(jnp.bfloat16)
-    send_own(1)
+    share_tokens()
+    gathered(0, 1)
+    tokens_before()
+    keys_of_both()
+    second_near(2, 2, 3)
+    first_near(4, 5)
+    gathered(2, 3)
+    values_of_both()
     landed(2, 2)
-    stage_one(6)
+    first_own(6)
     landed(6, 2)
-    stage_one(7)
+    first_own(7)
+    second_near(0, 4, 5)
+    first_far(4, 5)
+    second_own(6, 7)
     arrive(0, 0)
+    second_near(1, 4, 5)
+    second_near(3, 4, 5)
+    first_near(6, 7)
     arrive(1, 0)
-    for d in range(1, SIDE):
-        stage_two(4, d)
-        stage_two(5, d)
-    stage_two(6, 0)
-    stage_two(7, 0)
+    second_near(2, 4, 5)
+    relay(0)
+    second_near(0, 6, 7)
     arrive(0, 1)
+    relay(1)
+    first_far(6, 7)
+    gathered(4, 5)
     arrive(1, 1)
-    for d in range(1, SIDE):
-        stage_two(6, d)
-        stage_two(7, d)
+    project_queries(0)
+    second_near(1, 6, 7)
+    second_near(3, 6, 7)
+    attend_near(0)
     arrive(0, 2)
+    second_near(2, 6, 7)
+    attend_steps(0, (0, 1))
     arrive(1, 2)
+    gathered(6, 7)
+    project_queries(2)
+    attend_near(2)
     arrive(0, 3)
-    gathered(4)
-    gathered(5)
+    attend_steps(0, (2,))
+    attend_steps(2, (0, 1))
     arrive(1, 3)
-    project_queries(0)
-    attend(zl, 0, True)
-    attend_steps(0, (0, 1))
+    attend_steps(2, (2,))
+    wrapped(0)
+    wrapped(1)
+    attend_wrapped(0)
+    attend_wrapped(2)
+    attend_steps(0, (3,))
+    attend_steps(2, (3,))
     arrive(0, 4)
-    attend_steps(0, (2, 3))
     arrive(1, 4)
     attend_steps(0, (4,))
-    arrive(0, 5)
-    arrive(1, 5)
-    gathered(6)
-    gathered(7)
-    project_queries(2)
-    attend(zl, 2, True)
-    attend_steps(2, (0, 1, 2, 3))
-    arrive(0, 6)
-    attend_steps(2, (4, 5))
-    attend_steps(0, (5,))
-    arrive(1, 6)
-    attend_steps(2, (6,))
-    attend_steps(0, (6,))
+    attend_steps(2, (4,))
 
     for h in range(8):
         value = acc[h] * (1.0 / total[h])
@@ -393,13 +528,23 @@
 
     w_copy.wait_send()
     tok_copy.wait_send()
+
+    @pl.when(zl < LINE - 1)
+    def _():
+        prev_copy.wait_send()
+
+    @pl.when(zl > 0)
+    def _():
+        prev_share.wait_send()
+
     spread_done()
+    wrap_done()
     for g in range(len(GROUPS)):
         planes_done(g)
     for kind in range(2):
-        for s in range(LINE - 1):
-
-            @pl.when((zl >= s) & (zl < LINE - 1))
+        for s in range(STEPS):
+
+            @pl.when((zl > s) & (zl < LINE - 1))
             def _(kind=kind, s=s):
                 kv_copy(kind, s).wait_send()
 
@@ -413,7 +558,7 @@
     half = HEAD_DIM // 2
     frequency = rope_theta ** (-(jnp.arange(half).astype(jnp.float32) * 2.0) / HEAD_DIM)
     chip = lax.div(lax.axis_index("seq"), 2)
-    positions = (chip * 256 + jnp.arange(256)).astype(jnp.float32)
+    positions = (chip * 256 - 256 + jnp.arange(512)).astype(jnp.float32)
     angles = positions[:, None] * frequency[None, :]
     cosine, sine = jnp.cos(angles), jnp.sin(angles)
     cos = jnp.concatenate([cosine, cosine], axis=1)
@@ -433,6 +578,7 @@
             pltpu.VMEM((3, 64, 128), bf16),
             pltpu.VMEM((2048, 1536), bf16),
             pltpu.VMEM((256, 2048), bf16),
+            pltpu.VMEM((256, 2048), bf16),
             pltpu.VMEM((LINE, 2, 256, 128), bf16),
             pltpu.VMEM((LINE, 2, 128, 256), bf16),
             pltpu.VMEM((8, 128, 256), bf16),
@@ -440,8 +586,10 @@
             pltpu.VMEM((8, 1, 256), f32),
             pltpu.VMEM((8, 1, 256), f32),
             pltpu.VMEM((256, 1024), bf16),
-            dma((8,)), dma((3,)), dma((9,)), dma((24,)), dma((8,)), dma((24,)), dma((8,)),
-            dma((96,)), dma((14,)), dma((14,)),
+            pltpu.VMEM((2, 256, 128), bf16),
+            pltpu.VMEM((2, 128, 256), bf16),
+            dma((12,)), dma((3,)), dma((9,)), dma((24,)), dma((8,)), dma((32,)), dma((8,)),
+            dma((128,)), dma((2 * STEPS,)), dma((2 * STEPS,)), dma((4,)), dma((4,)),
         ],
         compiler_params=pltpu.CompilerParams(
             collective_id=0, has_side_effects=True, vmem_limit_bytes=48 * 1024 * 1024

time: 96.9 us -> 90.4 us (0.933)
  Pallas kernels: 92.5 us -> 86.1 us
    pallas_call x1, Pallas kernels: 92.5 us -> 86.1 us  [shards(): pl.pallas_call(kernel, name='gather_attend', out_shape=jax.ShapeDtypeStru...]
where the time goes in v3:
time: 90.4 us; the launch traced here: 90.2 us
  Pallas kernels  86.1 us (95%)
  other arithmetic  1.9 us (2%)
  local copies, waits for them, and re-layouts  1.49 us (2%)
    pallas_call x1, Pallas kernels, shards(): pl.pallas_call(kernel, name='gather_attend', out_shape=jax.ShapeDtypeStru...  86.1 us

profile of v3, /device:TPU:225, one launch (start us, length us, event | category | flops | bytes accessed | tf_op | source)
XLA Modules:
  0.0 90.2 jit_solution(4816110593222413941)
XLA Ops:
  0.7 1.0 %fusion = (f32[512,64]{1,0:T(8,128)S(1)}, f32[512,64]{1,0:T(8,128)S(1)}, f32[512,64]{1,0:T(8,128)S(1)}) fusion(f32[64]{0:T(128)S(1)} %multiply_power_fusion, f32[512]{0:T(512)S(1)} %add_convert_fusion), kind=kLoop, calls=%fused_computation.5 | loop fusion | flops 65536 | bytes 395520 | tf_op jit(solution)/shard_map/neg | solution.py:565
  1.7 0.0 copy-start.1
  1.7 0.0 copy-start.2
  1.7 0.0 copy-start.3
  1.7 0.0 copy-start.4
  1.7 0.0 copy-start
  1.7 0.2 pad_maximum_fusion
  1.9 0.6 copy-done.1
  2.5 0.0 copy-done.2
  2.5 0.0 copy-done.3
  2.6 0.0 copy-done.4
  2.6 0.7 fusion.7
  3.3 0.0 copy-done
  3.3 86.1 %gather_attend.1 = bf16[128,2048]{1,0:T(8,128)(2,1)S(1)} custom-call(bf16[128,2048]{1,0:T(8,128)(2,1)S(1)} %bitcast.3, bf16[64,192]{1,0:T(8,128)(2,1)S(1)} %get-tuple-element.2.shard, f32[512,128]{1,0:T(8,128)S(1)} %get-tuple-element.7.cos, f32[512,128]{1,0:T(8,128)S(1)} %get-tuple-element.8.sin), custom_call_target="tpu_custom_call" | custom-call | tf_op jit(solution)/shard_map/gather_attend/pallas_call | solution.py:570
  89.4 0.8 copy.8
  (2 shorter events, 0.0 us)
Async XLA Ops:
  1.7 0.8 copy-start.1
  1.7 0.9 copy-start.2
  1.7 0.9 copy-start.3
  1.7 0.9 %copy-start.4 = (f32[64,192]{1,0:T(8,128)S(1)}, f32[64,192]{1,0:T(8,128)}, u32[]{:S(2)}) copy-start(f32[64,192]{1,0:T(8,128)} %param.7) | copy-start | bytes 147460
  1.7 1.6 %copy-start = (bf16[1,128,2048]{2,1,0:T(8,128)(2,1)S(1)}, bf16[1,128,2048]{2,1,0:T(8,128)(2,1)}, u32[]{:S(2)}) copy-start(bf16[1,128,2048]{2,1,0:T(8,128)(2,1)} %param.5) | copy-start | bytes 1572868

commit v4 on v3

--- a/solution.py
+++ b/solution.py
@@ -34,7 +34,6 @@
     (0, 256, True), (512, 256, False), (256, 256, True), (768, 256, False),
 )
 COARSE = (8, 4, 12)
-FINE = (1, 15, 2)
 STEPS = 5
 POWER = SCALE / math.log(2.0)
 
@@ -126,6 +125,8 @@
             return local, (b >= HEADS) & (lax.rem(lax.div(past, 2), 2) == c)
         return lax.rem(b, 8), (b < HEADS) & (lax.div(b, 8) == c)
 
+    fine = (1, RING - 1, 2 + 12 * c)
+
     def z_send(src, where, send, recv, steps):
         for d in steps:
             remote(src, where, send, recv, at(x, y, lax.rem(z + d, RING), c)).start()
@@ -138,7 +139,7 @@
             def _(j=j, local=local):
                 where = place(zh, local * BLK)
                 sem = zrecv.at[local * 2 + zh]
-                z_send(blk.at[j], where, zsend.at[j], sem, COARSE + FINE)
+                z_send(blk.at[j], where, zsend.at[j], sem, COARSE + fine)
                 pltpu.make_async_copy(blk.at[j], where, sem).start()
 
     def pass_on(kind):
@@ -153,7 +154,7 @@
                     where = place(half, local * BLK)
                     sem = zrecv.at[local * 2 + half]
                     pltpu.make_async_copy(where, where, sem).wait()
-                    z_send(where, where, zpass.at[i * 3 + j], sem, FINE)
+                    z_send(where, where, zpass.at[i * 3 + j], sem, fine)
 
     def spread_done():
         for kind in (True, False):
@@ -291,11 +292,6 @@
         def _():
             ref = (values if kind else keys).at[0]
             pltpu.make_async_copy(ref, ref, wraprecv.at[2 + kind]).wait()
-
-    def attend_wrapped(offset):
-        @pl.when(zl == LINE - 1)
-        def _():
-            attend(0, offset, False)
 
     def wrap_done():
         for kind in range(2):
@@ -418,19 +414,68 @@
 
         lax.fori_loop(0, 2, group, 0)
 
+    def attend_many(slots, offset, first=False):
+        def group(i, carry):
+            for j in range(2):
+                h = i * 4 + offset + j
+                scores = [
+                    jnp.dot(keys[t, i], q[h], preferred_element_type=jnp.float32) for t in slots
+                ]
+                if first:
+                    row = lax.broadcasted_iota(jnp.int32, (256, 256), 0)
+                    column = lax.broadcasted_iota(jnp.int32, (256, 256), 1)
+                    scores[0] = jnp.where(row <= column, scores[0], -jnp.inf)
+                m = functools.reduce(jnp.maximum, scores)
+                m = jnp.max(m, axis=0, keepdims=True)
+                if not first:
+                    old = top[h]
+                    m = jnp.maximum(old, m)
+                parts = [jnp.exp2((one - m) * POWER) for one in scores]
+                mass = jnp.sum(functools.reduce(jnp.add, parts), axis=0, keepdims=True)
+                top[h] = m
+                if not first:
+                    shrink = jnp.exp2((old - m) * POWER)
+                    mass = mass + total[h] * shrink
+                total[h] = mass
+                result = None if first else acc[h] * shrink
+                for t, one in zip(slots, parts):
+                    part = jnp.dot(
+                        values[t, i], one.astype(jnp.bfloat16), preferred_element_type=jnp.float32
+                    )
+                    result = part if result is None else result + part
+                acc[h] = result
+            return carry
+
+        lax.fori_loop(0, 2, group, 0)
+
     def attend_near(offset):
-        attend(zl, offset, True)
+        @pl.when(zl == 0)
+        def _():
+            attend(zl, offset, True)
 
         @pl.when(zl > 0)
         def _():
-            attend(zl - 1, offset, False)
-
-    def attend_steps(offset, steps):
-        for s in steps:
-
-            @pl.when(zl > s + 1)
+            attend_many((zl, zl - 1), offset, True)
+
+    def attend_run(offset, steps):
+        @pl.when(zl > steps[-1] + 1)
+        def _():
+            attend_many([zl - 2 - s for s in steps], offset)
+
+        for s in steps[:-1]:
+
+            @pl.when((zl > s + 1) & (zl <= steps[-1] + 1))
             def _(s=s):
                 attend(zl - 2 - s, offset, False)
+
+    def attend_last(offset):
+        @pl.when(zl == LINE - 2)
+        def _():
+            attend(0, offset, False)
+
+        @pl.when(zl == LINE - 1)
+        def _():
+            attend_many((1, 0), offset)
 
     spread(True)
     spread(False)
@@ -494,26 +539,21 @@
     attend_near(0)
     arrive(0, 2)
     second_near(2, 6, 7)
-    attend_steps(0, (0, 1))
+    attend_run(0, (0, 1))
     arrive(1, 2)
     gathered(6, 7)
     project_queries(2)
     attend_near(2)
     arrive(0, 3)
-    attend_steps(0, (2,))
-    attend_steps(2, (0, 1))
     arrive(1, 3)
-    attend_steps(2, (2,))
+    attend_run(0, (2, 3))
+    attend_run(2, (0, 1, 2, 3))
     wrapped(0)
     wrapped(1)
-    attend_wrapped(0)
-    attend_wrapped(2)
-    attend_steps(0, (3,))
-    attend_steps(2, (3,))
     arrive(0, 4)
     arrive(1, 4)
-    attend_steps(0, (4,))
-    attend_steps(2, (4,))
+    attend_last(0)
+    attend_last(2)
 
     for h in range(8):
         value = acc[h] * (1.0 / total[h])

time: 90.4 us -> 83.4 us (0.923)
  the two profiles are of different devices: /device:TPU:225 before, /device:TPU:193 now
where the time goes in v4:
time: 83.4 us; the launch traced here: 83.3 us
  Pallas kernels  79.2 us (95%)
  other arithmetic  1.9 us (2%)
  local copies, waits for them, and re-layouts  1.49 us (2%)
    pallas_call x1, Pallas kernels, shards(): pl.pallas_call(kernel, name='gather_attend', out_shape=jax.ShapeDtypeStru...  79.2 us

profile of v4, /device:TPU:193, one launch (start us, length us, event | category | flops | bytes accessed | tf_op | source)
XLA Modules:
  0.0 83.3 jit_solution(247112401235147944)
XLA Ops:
  0.7 1.0 %fusion = (f32[512,64]{1,0:T(8,128)S(1)}, f32[512,64]{1,0:T(8,128)S(1)}, f32[512,64]{1,0:T(8,128)S(1)}) fusion(f32[64]{0:T(128)S(1)} %multiply_power_fusion, f32[512]{0:T(512)S(1)} %add_convert_fusion), kind=kLoop, calls=%fused_computation.5 | loop fusion | flops 65536 | bytes 395520 | tf_op jit(solution)/shard_map/neg | solution.py:605
  1.7 0.0 copy-start.1
  1.7 0.0 copy-start.2
  1.7 0.0 copy-start.3
  1.7 0.0 copy-start.4
  1.7 0.0 copy-start
  1.7 0.2 pad_maximum_fusion
  1.9 0.6 copy-done.1
  2.5 0.0 copy-done.2
  2.5 0.0 copy-done.3
  2.6 0.0 copy-done.4
  2.6 0.7 fusion.7
  3.3 0.0 copy-done
  3.3 79.2 %gather_attend.1 = bf16[128,2048]{1,0:T(8,128)(2,1)S(1)} custom-call(bf16[128,2048]{1,0:T(8,128)(2,1)S(1)} %bitcast.3, bf16[64,192]{1,0:T(8,128)(2,1)S(1)} %get-tuple-element.2.shard, f32[512,128]{1,0:T(8,128)S(1)} %get-tuple-element.7.cos, f32[512,128]{1,0:T(8,128)S(1)} %get-tuple-element.8.sin), custom_call_target="tpu_custom_call" | custom-call | tf_op jit(solution)/shard_map/gather_attend/pallas_call | solution.py:610
  82.5 0.8 copy.8
  (2 shorter events, 0.0 us)
Async XLA Ops:
  1.7 0.8 %copy-start.1 = (f32[64,192]{1,0:T(8,128)S(1)}, f32[64,192]{1,0:T(8,128)}, u32[]{:S(2)}) copy-start(f32[64,192]{1,0:T(8,128)} %param.6) | copy-start | bytes 147460
  1.7 0.9 %copy-start.2 = (f32[64,192]{1,0:T(8,128)S(1)}, f32[64,192]{1,0:T(8,128)}, u32[]{:S(2)}) copy-start(f32[64,192]{1,0:T(8,128)} %param.9) | copy-start | bytes 147460
  1.7 0.9 %copy-start.3 = (f32[64,192]{1,0:T(8,128)S(1)}, f32[64,192]{1,0:T(8,128)}, u32[]{:S(2)}) copy-start(f32[64,192]{1,0:T(8,128)} %param.8) | copy-start | bytes 147460
  1.7 0.9 %copy-start.4 = (f32[64,192]{1,0:T(8,128)S(1)}, f32[64,192]{1,0:T(8,128)}, u32[]{:S(2)}) copy-start(f32[64,192]{1,0:T(8,128)} %param.7) | copy-start | bytes 147460
  1.7 1.6 %copy-start = (bf16[1,128,2048]{2,1,0:T(8,128)(2,1)S(1)}, bf16[1,128,2048]{2,1,0:T(8,128)(2,1)}, u32[]{:S(2)}) copy-start(bf16[1,128,2048]{2,1,0:T(8,128)(2,1)} %param.5) | copy-start | bytes 1572868
